TPU v7x, 256 devices: a whole 4x4x8 slice. The times are simulated.
256 devices in a mesh: space: 32 (over y, z), chan: 8 (over x, core).
Axes of the slice: x: 4, y: 4, z: 8, core: 2. Of those that a mesh axis runs over, the one named last changes fastest.
Arguments:
- features: bfloat16 [65536, 256], P('space', 'chan'), may hold values from -6 to 6
- kernel_map: int32 [32, 27, 16, 3], P('space'), may hold values from 0 to 31, as said below
- block_count: int32 [32], replicated, may hold values from 3 to 16, as said below
- weight_one: bfloat16 [27, 256, 256], P(None, 'chan'), may hold values from -0.078125 to 0.078125
- weight_two: bfloat16 [27, 256, 256], P(None, 'chan'), may hold values from -0.078125 to 0.078125
- cotangent: bfloat16 [65536, 256], P('space', 'chan'), may hold values from -0.026977539 to 0.026977539
Outputs:
- output: bfloat16 [65536, 256], P('space', 'chan')
- grad_one: float32 [27, 256, 256], P(None, 'chan', 'space')
- grad_two: float32 [27, 256, 256], P(None, 'chan', 'space')
Inputs may be any that keep to these rules, and one draw needn't show every extreme that they name: `kernel_map`: column 0 of slab s's entries is s - 1, s or s + 1. Column 1 is a block below block_count of that source slab; from slab s - 1 it is one of that slab's last 2 live blocks, from slab s + 1 one of its first 2. Column 2 lies below 16. Entries stand in offset order, 16 per offset and slab. `block_count`: at least one slab has all 16 blocks live.
All inputs are finite; a program needn't handle non-finite values.
Results may differ from a plain program's by a relative error of at most 0.015.
Values may be sent and summed in bfloat16 or wider, within the bound.
A program may use at most 64 MiB of HBM per device.

v0:
```python
import jax
import jax.numpy as jnp
from jax import lax
from jax.sharding import PartitionSpec as P

BLK = 128
HB = 2


def padded(shard, sides, width):
    for axis, dim in sides:
        size, length = (lax.axis_size(axis), shard.shape[dim])
        up = [(i, (i + 1) % size) for i in range(size - 1)]
        down = [(j, i) for i, j in up]
        last = lax.slice_in_dim(shard, length - width, length, axis=dim)
        leading = lax.slice_in_dim(shard, 0, width, axis=dim)
        before = lax.ppermute(last, axis, up)
        after = lax.ppermute(leading, axis, down)
        shard = jnp.concatenate([before, shard, after], axis=dim)
    return shard


def local(features, kernel_map, block_count, weight_one, weight_two, cotangent):
    shard = lax.axis_index("space")
    nblocks = features.shape[0] // BLK
    own_count = block_count[shard]
    left_count = block_count[jnp.maximum(shard - 1, 0)]
    entries = kernel_map[0]
    source = entries[..., 0]
    inblock = entries[..., 1]
    target = entries[..., 2]
    position = jnp.where(
        source == shard,
        HB + inblock,
        jnp.where(source < shard, inblock - (left_count - HB), HB + nblocks + inblock),
    )
    live = target < own_count
    select = (target[..., None] == jnp.arange(nblocks, dtype=jnp.int32)) & live[..., None]
    select_f = select.astype(jnp.float32)
    select_b = select.astype(jnp.bfloat16)
    place = (
        (position[..., None] == jnp.arange(nblocks + 2 * HB, dtype=jnp.int32)) & live[..., None]
    ).astype(jnp.float32)

    def widen(feat):
        return lax.all_gather(feat, "chan", axis=1, tiled=True)

    def attach_rims(feat):
        width = feat.shape[1]
        cube = feat.reshape(nblocks, BLK, width)
        first = cube[:HB]
        last = lax.dynamic_slice_in_dim(cube, own_count - HB, HB, 0)
        rims = jnp.concatenate([first, last], 0).reshape(2 * HB * BLK, width)
        outer = padded(rims, (("space", 0),), HB * BLK)
        return jnp.concatenate([outer[: HB * BLK], feat, outer[3 * HB * BLK :]], 0)

    def extend(feat):
        return attach_rims(widen(feat))

    def convolve(wide, weights):
        cube = wide.reshape(-1, BLK, wide.shape[1])

        def convolve_add_offset(total, item):
            index, choose, kernel = item
            picked = cube[index]
            prod = jnp.einsum("erc,dc->erd", picked, kernel, preferred_element_type=jnp.float32)
            return (total + jnp.einsum("eb,erd->brd", choose, prod), None)

        start = jnp.zeros((nblocks, BLK, weights.shape[1]), jnp.float32)
        total, _ = lax.scan(convolve_add_offset, start, (position, select_f, weights))
        return total.reshape(nblocks * BLK, weights.shape[1])

    def weight_grad(wide, grads_cube):
        cube = wide.reshape(-1, BLK, wide.shape[1])

        def one_offset(item):
            index, choose = item
            picked = cube[index]
            chosen = jnp.einsum(
                "eb,brd->erd", choose, grads_cube, preferred_element_type=jnp.float32
            ).astype(jnp.bfloat16)
            return jnp.einsum("erc,erd->dc", picked, chosen, preferred_element_type=jnp.float32)

        return lax.map(one_offset, (position, select_b))

    wide_x = extend(features)
    z_one = convolve(wide_x, weight_one)
    hidden = jax.nn.silu(z_one).astype(jnp.bfloat16)
    wide_h = extend(hidden)
    output = convolve(wide_h, weight_two).astype(jnp.bfloat16)
    grad_cube = cotangent.reshape(nblocks, BLK, -1)
    grad_two = weight_grad(wide_h, grad_cube)
    width = cotangent.shape[1]

    def spread_add_offset(total, item):
        choose, spot, kernel = item
        chosen = jnp.einsum(
            "eb,brd->erd", choose, grad_cube, preferred_element_type=jnp.float32
        ).astype(jnp.bfloat16)
        contrib = jnp.einsum("erd,dc->erc", chosen, kernel, preferred_element_type=jnp.float32)
        return (total + jnp.einsum("ex,erc->xrc", spot, contrib), None)

    start = jnp.zeros((nblocks + 2 * HB, BLK, weight_two.shape[2]), jnp.float32)
    total, _ = lax.scan(spread_add_offset, start, (select_b, place, weight_two))
    partial_value = total.reshape((nblocks + 2 * HB) * BLK, weight_two.shape[2])
    summed = lax.psum_scatter(partial_value, "chan", scatter_dimension=1, tiled=True)
    width = summed.shape[1]
    cube = summed.reshape(-1, BLK, width)
    edges = jnp.concatenate([cube[:HB], cube[HB + nblocks :]], 0).reshape(2 * HB * BLK, width)
    back = padded(edges, (("space", 0),), HB * BLK)
    inner = cube[HB : HB + nblocks]
    from_left = back[: HB * BLK].reshape(HB, BLK, width)
    from_right = back[3 * HB * BLK :].reshape(HB, BLK, width)
    inner = inner.at[:HB].add(from_left)
    tail = lax.dynamic_slice_in_dim(inner, own_count - HB, HB, 0) + from_right
    inner = lax.dynamic_update_slice_in_dim(inner, tail, own_count - HB, 0)
    grad_hidden = inner.reshape(nblocks * BLK, width)
    gate = jax.nn.sigmoid(z_one)
    grad_z = (grad_hidden * gate * (1.0 + z_one * (1.0 - gate))).astype(jnp.bfloat16)
    grad_one = weight_grad(wide_x, grad_z.reshape(nblocks, BLK, -1))
    totals = (
        lax.psum_scatter(grad_one, "space", scatter_dimension=2, tiled=True),
        lax.psum_scatter(grad_two, "space", scatter_dimension=2, tiled=True),
    )
    return (output, totals[0], totals[1])


def solution(mesh):
    return jax.shard_map(
        local,
        mesh=mesh,
        in_specs=(
            P("space", "chan"),
            P("space", None, None, None),
            P(),
            P(None, "chan", None),
            P(None, "chan", None),
            P("space", "chan"),
        ),
        out_specs=(P("space", "chan"), P(None, "chan", "space"), P(None, "chan", "space")),
        check_vma=False,
    )
```

profile of v0, /device:TPU:4, one launch (start us, length us, event | category | flops | bytes accessed | tf_op | source)
XLA Modules:
  0.0 890.1 jit_solution(15789710916156473926)
XLA Ops:
  14.6 22.7 %all-gather.3.cloned.1.call-done = bf16[2048,256]{0,1:T(8,128)(2,1)} async-done(((bf16[2048,32]{0,1:T(8,128)(2,1)}), bf16[2048,256]{0,1:T(8,128)(2,1)}) %all-gather.3.cloned.1.call-update) | async-done | bytes 1048592 | tf_op jit(solution)/shard_map/all_gather | solution.py:46
  39.1 3.5 collective-permute-start
  45.7 4.2 collective-permute-done.1
  53.5 173.4 %while.56 = (s32[]{:T(128)}, f32[16,128,32]{1,0,2:T(8,128)}, bf16[27,16,16]{1,2,0:T(8,128)(2,1)}, s32[27,16]{1,0:T(8,128)S(1)}, bf16[20,128,256]{2,1,0:T(8,128)(...) while((s32[]{:T(128)}, f32[16,128,32]{1,0,2:T(8,128)}, ...), condition=%wide.region_1.2_spmd.clone, body=%wide.region_0.1_spmd.clone.sunk | while | flops 35783728 | bytes 3958115 | solution.py:70
  53.5 2.9 gather_fusion.2
  59.6 2.9 gather_fusion.2
  66.1 2.9 gather_fusion.2
  72.5 2.9 gather_fusion.2
  78.9 2.9 gather_fusion.2
  91.8 2.9 gather_fusion.2
  98.2 2.9 gather_fusion.2
  104.7 2.9 gather_fusion.2
  111.1 2.9 gather_fusion.2
  124.0 2.9 gather_fusion.2
  130.4 2.9 gather_fusion.2
  136.8 2.9 gather_fusion.2
  143.3 2.9 gather_fusion.2
  149.7 2.9 gather_fusion.2
  156.1 2.9 gather_fusion.2
  162.6 2.9 gather_fusion.2
  228.7 108.4 %while.58 = (s32[]{:T(128)}, f32[20,128,256]{2,0,1:T(8,128)S(1)}, bf16[27,16,20]{2,1,0:T(8,128)(2,1)}, bf16[27,16,16]{2,1,0:T(8,128)(2,1)S(1)}, bf16[16,128,32]{...) while((s32[]{:T(128)}, f32[20,128,256]{2,0,1:T(8,128)S(1)}, ...), condition=%wide.region_5.6_spmd.clone, body=%wide.region_4.5_spmd.clone.sunk | while | flops 57999360 | bytes 6317155 | solution.py:104
  339.5 3.2 copy.71
  344.4 3.5 collective-permute-start.2
  350.3 4.9 collective-permute-done.3
  355.3 21.4 %reduce-scatter.10.cloned.1.call-done = f32[32,2560]{1,0:T(8,128)} async-done(((f32[256,2560]{1,0:T(8,128)}), f32[32,2560]{1,0:T(8,128)}) %reduce-scatter.10.cloned.1.call-update) | async-done | bytes 327696
  378.3 4.1 collective-permute-start.4
  385.5 64.0 %while.55 = (s32[]{:T(128)}, f32[27,32,256]{2,1,0:T(8,128)}, bf16[27,16,16]{2,1,0:T(8,128)(2,1)S(1)}, bf16[16,128,32]{1,0,2:T(8,128)(2,1)S(1)}, s32[27,16]{1,0:T...) while((s32[]{:T(128)}, f32[27,32,256]{2,1,0:T(8,128)}, bf16[27,16,16]{2,1,0:T(8,128)(2,1)S(1)}, ...), condition=%wide.region_11.12_spmd, body=%wide.region_10.11_spmd.sunk | while | flops 35718192 | bytes 3580757 | solution.py:84
  449.5 3.4 copy.69
  462.4 141.8 %while.54 = (s32[]{:T(128)}, f32[27,32,256]{2,1,0:T(8,128)}, bf16[27,16,16]{2,1,0:T(8,128)(2,1)}, bf16[16,128,32]{1,0,2:T(8,128)(2,1)S(1)}, s32[27,16]{1,0:T(8,1...) while((s32[]{:T(128)}, f32[27,32,256]{2,1,0:T(8,128)}, bf16[27,16,16]{2,1,0:T(8,128)(2,1)}, ...), condition=%wide.region_8.9_spmd, body=%wide.region_7.8_spmd.sunk | while | flops 35718192 | bytes 3581265 | solution.py:84
  604.3 3.4 copy.68
  607.6 91.3 %while.57 = (s32[]{:T(128)}, f32[16,128,32]{1,0,2:T(8,128)S(1)}, bf16[27,16,16]{1,2,0:T(8,128)(2,1)}, s32[27,16]{1,0:T(8,128)}, bf16[20,128,256]{2,1,0:T(8,128)(...) while((s32[]{:T(128)}, f32[16,128,32]{1,0,2:T(8,128)S(1)}, ...), condition=%wide.region_3.4_spmd.clone, body=%wide.region_2.3_spmd.clone.sunk | while | flops 35783728 | bytes 3958115 | solution.py:70
  699.6 184.0 %reduce-scatter.6.cloned.1.call-done = f32[27,32,8]{1,2,0:T(8,128)} async-done(((f32[27,32,256]{1,2,0:T(8,128)}), f32[27,32,8]{1,2,0:T(8,128)}) %reduce-scatter.6.cloned.1.call-update) | async-done | bytes 27664 | tf_op jit(solution)/shard_map/reduce_scatter | solution.py:122
  (677 shorter events, 566.0 us)
Async XLA Ops:
  7.2 30.2 %all-gather.3.cloned.1.call-start = ((), (), s32[]{:S(2)}) async-start(), calls=%async_computation.3 | async-start | bytes 1179648 | tf_op jit(solution)/shard_map/all_gather | solution.py:46
  7.9 334.9 %all-gather.5.cloned.1.call-start = ((), (), s32[]{:S(2)}) async-start(), calls=%async_computation.4 | async-start | bytes 1179648 | tf_op jit(solution)/shard_map/all_gather | solution.py:46
  37.3 5.2 copy-start.2
  39.1 6.6 collective-permute-start
  42.6 7.2 collective-permute-start.1
  226.9 1.8 copy-start.5
  228.7 148.1 %reduce-scatter.10.cloned.1.call-start = ((), (), s32[]{:S(2)}) async-start(), calls=%async_computation.7 | async-start | bytes 2949120
  342.8 356.9 %reduce-scatter.8.cloned.1.call-start = ((), (), s32[]{:S(2)}) async-start(), calls=%async_computation.6 | async-start | bytes 3649536 | tf_op jit(solution)/shard_map/reduce_scatter | solution.py:123
  344.4 6.0 collective-permute-start.2
  347.8 7.4 collective-permute-start.3
  378.3 79.2 %collective-permute-start.4 = (f32[256,32]{1,0:T(8,128)}, f32[256,32]{1,0:T(8,128)}, u32[]{:S(2)}, u32[]{:S(2)}) collective-permute-start(f32[256,32]{1,0:T(8,128)} %copy.75), channel_id=1, source_target_pairs={{0,8},{8,16},{16,24},{24,32},{32,40},{40,48},{48,56},{56,64},{64,7... | collective-permute-start | bytes 98312 | tf_op jit(solution)/shard_map/ppermute | solution.py:17
  383.2 76.1 %collective-permute-start.5 = (f32[256,32]{1,0:T(8,128)}, f32[256,32]{1,0:T(8,128)}, u32[]{:S(2)}, u32[]{:S(2)}) collective-permute-start(f32[256,32]{1,0:T(8,128)} %copy.76), channel_id=1, source_target_pairs={{8,0},{16,8},{24,16},{32,24},{40,32},{48,40},{56,48},{64,56},{72,6... | collective-permute-start | bytes 98312 | tf_op jit(solution)/shard_map/ppermute | solution.py:18
  449.5 3.4 copy-start.3
  452.9 1.0 copy-start.4
  452.9 8.4 copy-start.1
  452.9 430.6 %reduce-scatter.6.cloned.1.call-start = ((), (), s32[]{:S(2)}) async-start(), calls=%async_computation.5 | async-start | bytes 3649536 | tf_op jit(solution)/shard_map/reduce_scatter | solution.py:122
  453.9 8.6 copy-start
Sparse Core Ops, SparseCore 0:
  9.9 27.4 all-gather.2
  228.8 25.9 all-gather.4
  342.9 33.8 reduce-scatter.9
  453.0 216.3 reduce-scatter.7
  674.3 209.1 reduce-scatter.5
where the time goes:
time: 900 us; the launch traced here: 890 us
  matrix products  331 us (37%)
  waiting for transfers between devices  240 us (27%)
  local copies, waits for them, and re-layouts  223 us (25%)
  other arithmetic  62.2 us (7%)
  between operations  16 us (2%)
  starting transfers between devices  15.1 us (2%)
    reduce_scatter x1, waiting for transfers between devices, local(): lax.psum_scatter(grad_one, 'space', scatter_dimension=2, tiled=True)  184 us
    gather x54, local copies, waits for them, and re-layouts, convolve_add_offset(): picked = cube[index]  96.1 us
    dot_general x54, matrix products, one_offset(): jnp.einsum('erc,erd->dc', picked, chosen, preferred_element_type=jnp.floa...  81.2 us
    dot_general x54, matrix products, convolve_add_offset(): jnp.einsum('erc,dc->erd', picked, kernel, preferred_element_type=jnp.floa...  74.3 us
    dot_general x54, matrix products, convolve_add_offset(): return (total + jnp.einsum('eb,erd->brd', choose, prod), None)  73.9 us
    dot_general x27, matrix products, spread_add_offset(): return (total + jnp.einsum('ex,erc->xrc', spot, contrib), None)  69.9 us
    gather x54, local copies, waits for them, and re-layouts, one_offset(): picked = cube[index]  59.5 us
    select_n x54, other arithmetic, one_offset(): picked = cube[index]  36.8 us
  transfers between devices with their start and end apart: 11, of which 7 were waited for; matrix products, arithmetic and copies ran while one was open for 49% of the time, Pallas kernels for 0%

commit v1 on v0

--- a/solution.py
+++ b/solution.py
@@ -43,7 +43,9 @@
     ).astype(jnp.float32)
 
     def widen(feat):
-        return lax.all_gather(feat, "chan", axis=1, tiled=True)
+        return jnp.concatenate(
+            lax.all_to_all(jnp.stack([feat] * lax.axis_size("chan")), "chan", 0, 0), axis=1
+        )
 
     def attach_rims(feat):
         width = feat.shape[1]

time: 900 us -> 808 us (0.90)
  other arithmetic: 62.2 us -> 9.08 us
  local copies, waits for them, and re-layouts: 223 us -> 190 us
  matrix products: 331 us -> 307 us
  blocking collectives: 0 us -> 18.5 us
  waiting for transfers between devices: 240 us -> 230 us
    gather x54, local copies, waits for them, and re-layouts: 96.1 us -> 33.2 us  [convolve_add_offset(): picked = cube[index]]
    dot_general x54, matrix products: 73.9 us -> 31.2 us  [convolve_add_offset(): return (total + jnp.einsum('eb,erd->brd', choose, prod), None)]
    select_n x54, other arithmetic: 36.8 us -> 0.4 us  [one_offset(): picked = cube[index]]
    dot_general x54, matrix products: 81.2 us -> 114 us  [one_offset(): jnp.einsum('erc,erd->dc', picked, chosen, preferred_element_type=jnp.floa...]
    reduce_scatter x1, waiting for transfers between devices: 184 us -> 214 us  [local(): lax.psum_scatter(grad_one, 'space', scatter_dimension=2, tiled=True)]
    gather x54, local copies, waits for them, and re-layouts: 59.5 us -> 86 us  [one_offset(): picked = cube[index]]
    all_gather x2 -> x0, waiting for transfers between devices: 22.7 us -> none  [widen(): return lax.all_gather(feat, 'chan', axis=1, tiled=True)]
    unnamed x6 -> x4, waiting for transfers between devices: 22.1 us -> 0.07 us
  transfers between devices with their start and end apart: 11 -> 10, of which waited for: 7 -> 5; matrix products, arithmetic and copies ran while one was open for 49% -> 62% of each run, Pallas kernels for 0% -> 0%
where the time goes in v1:
time: 808 us; the launch traced here: 800 us
  matrix products  307 us (38%)
  waiting for transfers between devices  230 us (28%)
  local copies, waits for them, and re-layouts  190 us (24%)
  starting transfers between devices  22.9 us (3%)
  blocking collectives  18.5 us (2%)
  between operations  17.7 us (2%)
  other arithmetic  9.08 us (1%)
    reduce_scatter x1, waiting for transfers between devices, local(): lax.psum_scatter(grad_one, 'space', scatter_dimension=2, tiled=True)  214 us
    dot_general x54, matrix products, one_offset(): jnp.einsum('erc,erd->dc', picked, chosen, preferred_element_type=jnp.floa...  114 us
    gather x54, local copies, waits for them, and re-layouts, one_offset(): picked = cube[index]  86 us
    dot_general x27, matrix products, spread_add_offset(): return (total + jnp.einsum('ex,erc->xrc', spot, contrib), None)  69.8 us
    dot_general x54, matrix products, convolve_add_offset(): jnp.einsum('erc,dc->erd', picked, kernel, preferred_element_type=jnp.floa...  60.7 us
    convert_element_type x27, local copies, waits for them, and re-layouts, spread_add_offset(): chosen = jnp.einsum('eb,brd->erd', choose, grad_cube, preferred_element_t...  33.6 us
    gather x54, local copies, waits for them, and re-layouts, convolve_add_offset(): picked = cube[index]  33.2 us
    dot_general x54, matrix products, convolve_add_offset(): return (total + jnp.einsum('eb,erd->brd', choose, prod), None)  31.2 us
  transfers between devices with their start and end apart: 10, of which 5 were waited for; matrix products, arithmetic and copies ran while one was open for 62% of the time, Pallas kernels for 0%

profile of v1, /device:TPU:4, one launch (start us, length us, event | category | flops | bytes accessed | tf_op | source)
XLA Modules:
  0.0 799.6 jit_solution(11205785583324969650)
XLA Ops:
  10.1 6.4 all-to-all-start
  20.8 8.5 %all-to-all-done = bf16[8,2048,32]{1,2,0:T(8,128)(2,1)} async-done(((bf16[8,2048,32]{1,2,0:T(8,128)(2,1)}), bf16[8,2048,32]{1,2,0:T(8,128)(2,1)}, u32[]{:S(2)}, u32[]{:S(2)}) %all-to-all-start) | async-done | bytes 1048608 | tf_op jit(solution)/shard_map/all_to_all | solution.py:47
  31.7 2.9 collective-permute-start
  37.5 108.5 %while.58 = (s32[]{:T(128)}, f32[20,128,256]{2,0,1:T(8,128)S(1)}, bf16[27,16,20]{2,1,0:T(8,128)(2,1)}, bf16[27,16,16]{2,1,0:T(8,128)(2,1)S(1)}, bf16[16,128,32]{...) while((s32[]{:T(128)}, f32[20,128,256]{2,0,1:T(8,128)S(1)}, ...), condition=%wide.region_5.6_spmd.clone, body=%wide.region_4.5_spmd.clone.sunk | while | flops 57999360 | bytes 6317155 | solution.py:106
  38.9 2.6 select_add_fusion.2
  42.9 2.6 select_add_fusion.2
  46.9 2.6 select_add_fusion.2
  50.9 2.6 select_add_fusion.2
  55.0 2.6 select_add_fusion.2
  67.0 2.6 select_add_fusion.2
  79.1 2.6 select_add_fusion.2
  83.1 2.6 select_add_fusion.2
  87.1 2.6 select_add_fusion.2
  91.1 2.6 select_add_fusion.2
  99.2 2.6 select_add_fusion.2
  111.2 2.6 select_add_fusion.2
  115.2 2.6 select_add_fusion.2
  119.3 2.6 select_add_fusion.2
  123.3 2.6 select_add_fusion.2
  131.3 2.6 select_add_fusion.2
  148.3 3.2 copy.67
  153.8 55.1 %while.56 = (s32[]{:T(128)}, f32[16,128,32]{1,0,2:T(8,128)S(1)}, bf16[27,16,16]{1,2,0:T(8,128)(2,1)S(1)}, s32[27,16]{1,0:T(8,128)S(1)}, bf16[20,128,256]{2,1,0:T...) while((s32[]{:T(128)}, f32[16,128,32]{1,0,2:T(8,128)S(1)}, ...), condition=%wide.region_1.2_spmd.clone, body=%wide.region_0.1_spmd.clone.sunk | while | flops 35783728 | bytes 3957607 | solution.py:72
  209.7 18.5 %all_to_all.10 = bf16[8,2048,32]{1,2,0:T(8,128)(2,1)S(1)} all-to-all(bf16[8,2048,32]{1,2,0:T(8,128)(2,1)S(1)} %stack.5), channel_id=1, replica_groups=mesh['space'=32,'chan'=8] {'chan'}, dimensions={0} | all-to-all | bytes 2097152 | tf_op jit(solution)/shard_map/all_to_all | solution.py:47
  228.7 4.5 collective-permute-start.2
  236.0 5.0 collective-permute-done.3
  246.0 5.1 collective-permute-start.4
  254.2 104.9 %while.55 = (s32[]{:T(128)}, f32[27,32,256]{2,1,0:T(8,128)}, bf16[27,16,16]{2,1,0:T(8,128)(2,1)S(1)}, bf16[16,128,32]{1,0,2:T(8,128)(2,1)S(1)}, s32[27,16]{1,0:T...) while((s32[]{:T(128)}, f32[27,32,256]{2,1,0:T(8,128)}, bf16[27,16,16]{2,1,0:T(8,128)(2,1)S(1)}, ...), condition=%wide.region_11.12_spmd, body=%wide.region_10.11_spmd.sunk | while | flops 35718192 | bytes 3580757 | solution.py:86
  359.0 3.3 copy.66
  375.3 123.3 %while.54 = (s32[]{:T(128)}, f32[27,32,256]{2,1,0:T(8,128)}, bf16[27,16,16]{2,1,0:T(8,128)(2,1)}, bf16[16,128,32]{1,0,2:T(8,128)(2,1)S(1)}, s32[27,16]{1,0:T(8,1...) while((s32[]{:T(128)}, f32[27,32,256]{2,1,0:T(8,128)}, bf16[27,16,16]{2,1,0:T(8,128)(2,1)}, ...), condition=%wide.region_8.9_spmd, body=%wide.region_7.8_spmd.sunk | while | flops 35718192 | bytes 3581265 | solution.py:86
  498.6 3.3 copy.65
  502.0 73.4 %while.57 = (s32[]{:T(128)}, f32[16,128,32]{1,0,2:T(8,128)S(1)}, bf16[27,16,16]{1,2,0:T(8,128)(2,1)}, s32[27,16]{1,0:T(8,128)S(1)}, bf16[20,128,256]{2,1,0:T(8,1...) while((s32[]{:T(128)}, f32[16,128,32]{1,0,2:T(8,128)S(1)}, ...), condition=%wide.region_3.4_spmd.clone, body=%wide.region_2.3_spmd.clone.sunk | while | flops 35783728 | bytes 3958115 | solution.py:72
  578.1 214.0 %reduce-scatter.6.cloned.1.call-done = f32[27,32,8]{1,2,0:T(8,128)} async-done(((f32[27,32,256]{1,2,0:T(8,128)}), f32[27,32,8]{1,2,0:T(8,128)}) %reduce-scatter.6.cloned.1.call-update) | async-done | bytes 27664 | tf_op jit(solution)/shard_map/reduce_scatter | solution.py:124
  (676 shorter events, 461.7 us)
Async XLA Ops:
  8.0 8.5 %copy-start.3 = (s32[1,27,16,3]{1,2,3,0:T(8,128)S(1)}, s32[1,27,16,3]{1,2,3,0:T(8,128)}, u32[]{:S(2)}) copy-start(s32[1,27,16,3]{1,2,3,0:T(8,128)} %param.19) | copy-start | bytes 15556
  8.0 8.5 %copy-start.2 = (bf16[2048,32]{0,1:T(8,128)(2,1)S(1)}, bf16[2048,32]{0,1:T(8,128)(2,1)}, u32[]{:S(2)}) copy-start(bf16[2048,32]{0,1:T(8,128)(2,1)} %param.23) | copy-start | bytes 393220
  8.0 8.6 %copy-start.4 = (s32[32]{0:T(128)S(1)}, s32[32]{0:T(128)}, u32[]{:S(2)}) copy-start(s32[32]{0:T(128)} %param.20) | copy-start | bytes 388
  10.1 19.3 %all-to-all-start = ((bf16[8,2048,32]{1,2,0:T(8,128)(2,1)}), bf16[8,2048,32]{1,2,0:T(8,128)(2,1)}, u32[]{:S(2)}, u32[]{:S(2)}) async-start(bf16[8,2048,32]{1,2,0:T(8,128)(2,1)} %stack.4), calls=%async_computation | async-start | bytes 2097152 | tf_op jit(solution)/shard_map/all_to_all | solution.py:47
  16.5 227.3 %reduce-scatter.10.cloned.1.call-start = ((), (), s32[]{:S(2)}) async-start(), calls=%async_computation.7 | async-start | bytes 2949120
  31.7 120.1 %collective-permute-start = (bf16[256,256]{0,1:T(8,128)(2,1)}, bf16[256,256]{0,1:T(8,128)(2,1)}, u32[]{:S(2)}, u32[]{:S(2)}) collective-permute-start(bf16[256,256]{0,1:T(8,128)(2,1)} %bitcast.159), channel_id=1, source_target_pairs={{0,8},{8,16},{16,24},{24,32},{32,40},{40,48},{48,56},{56,64},{64,7... | collective-permute-start | bytes 393224 | tf_op jit(solution)/shard_map/ppermute | solution.py:17
  36.2 115.6 %collective-permute-start.1 = (bf16[256,256]{0,1:T(8,128)(2,1)}, bf16[256,256]{0,1:T(8,128)(2,1)}, u32[]{:S(2)}, u32[]{:S(2)}) collective-permute-start(bf16[256,256]{0,1:T(8,128)(2,1)} %bitcast.20), channel_id=1, source_target_pairs={{8,0},{16,8},{24,16},{32,24},{40,32},{48,40},{56,48},{64,56},{72,6... | collective-permute-start | bytes 393224 | tf_op jit(solution)/shard_map/ppermute | solution.py:18
  151.5 426.6 %reduce-scatter.8.cloned.1.call-start = ((), (), s32[]{:S(2)}) async-start(), calls=%async_computation.6 | async-start | bytes 3649536 | tf_op jit(solution)/shard_map/reduce_scatter | solution.py:125
  208.8 0.7 copy-start.1
  228.7 7.3 collective-permute-start.2
  233.9 7.1 collective-permute-start.3
  246.0 121.9 %collective-permute-start.4 = (f32[256,32]{1,0:T(8,128)}, f32[256,32]{1,0:T(8,128)}, u32[]{:S(2)}, u32[]{:S(2)}) collective-permute-start(f32[256,32]{1,0:T(8,128)} %copy.71), channel_id=1, source_target_pairs={{0,8},{8,16},{16,24},{24,32},{32,40},{40,48},{48,56},{56,64},{64,7... | collective-permute-start | bytes 98312 | tf_op jit(solution)/shard_map/ppermute | solution.py:17
  251.8 117.0 %collective-permute-start.5 = (f32[256,32]{1,0:T(8,128)}, f32[256,32]{1,0:T(8,128)}, u32[]{:S(2)}, u32[]{:S(2)}) collective-permute-start(f32[256,32]{1,0:T(8,128)} %copy.72), channel_id=1, source_target_pairs={{8,0},{16,8},{24,16},{32,24},{40,32},{48,40},{56,48},{64,56},{72,6... | collective-permute-start | bytes 98312 | tf_op jit(solution)/shard_map/ppermute | solution.py:18
  359.0 3.4 copy-start
  362.4 429.7 %reduce-scatter.6.cloned.1.call-start = ((), (), s32[]{:S(2)}) async-start(), calls=%async_computation.5 | async-start | bytes 3649536 | tf_op jit(solution)/shard_map/reduce_scatter | solution.py:124
Sparse Core Ops, SparseCore 0:
  151.7 37.3 reduce-scatter.9
Sparse Core Ops, SparseCore 1:
  362.5 215.5 reduce-scatter.7
  583.0 209.1 reduce-scatter.5
